TPU v7x, 256 devices: a whole 4x4x8 slice. The times are simulated.
256 devices in a mesh: leaf: 64 (over y, z, core), rows: 4 (over x).
Axes of the slice: x: 4, y: 4, z: 8, core: 2. Of those that a mesh axis runs over, the one named last changes fastest.
Arguments:
- mixing: bfloat16 [192, 1024, 1024], P('leaf'), may hold values from 0.04 to 2048
- emission: bfloat16 [192, 256, 1024], P('leaf'), may hold values from 0.099609375 to 10
- prior: float32 [1024], replicated, may hold values from 0.1 to 10
- parent: int32 [192], P('leaf'), may hold values from -1 to 191, as said below
- observed: int32 [192, 512], P('leaf', 'rows'), may hold values from 0 to 255
Outputs:
- pair_counts: bfloat16 [192, 1024, 1024], P('leaf', 'rows')
- emit_counts: bfloat16 [192, 256, 1024], P('leaf', None, 'rows')
Inputs may be any that keep to these rules, and one draw needn't show every extreme that they name: Nodes are numbered 3 to an index of leaf, in order. Every parent has a smaller number than its child. A node that is not the first of its index of leaf has its parent among the nodes of the same index. The first node of index d > 0 has as parent the first node of index d with its lowest set binary digit cleared. Node 0 is the root.
All inputs are finite; a program needn't handle non-finite values.
Results may differ from a plain program's by a relative error of at most 0.009.
Values may be sent and summed in bfloat16 or wider, within the bound.
A program may use at most 128 MiB of HBM per device.

v0:
```python
import jax
import jax.numpy as jnp
from jax import lax
from jax.sharding import PartitionSpec as P


def from_partner(value, axis, bit):
    mask = 2**bit
    pairs = [(source, source ^ mask) for source in range(lax.axis_size(axis))]
    return lax.ppermute(value, axis, pairs)


def in_blocks(array, dim, count):
    lengths = array.shape
    pieces = array.reshape(*lengths[:dim], count, lengths[dim] // count, *lengths[dim + 1 :])
    return jnp.moveaxis(pieces, dim, 0)


def sum_at_owner(array, axis, dim):
    count = lax.axis_size(axis)
    pieces = lax.all_to_all(in_blocks(array, dim, count), axis, 0, 0, tiled=True)
    return jnp.sum(pieces.astype(jnp.float32), axis=0)


def lift(raw, weight):
    scale = jnp.mean(raw, axis=1, keepdims=True)
    lam = (raw / scale).astype(jnp.bfloat16)
    msg = lax.dot_general(lam, weight, (((1,), (1,)), ((), ())), preferred_element_type=jnp.float32)
    return (lam, msg)


def settle(q_par, lam, msg, weight):
    ratio = (q_par / msg).astype(jnp.bfloat16)
    post = lam.astype(jnp.float32) * jnp.dot(ratio, weight, preferred_element_type=jnp.float32)
    return (ratio, post)


def per_device(mixing, emission, prior, parent, observed):
    node_count = mixing.shape[0]
    states = mixing.shape[1]
    row_count = observed.shape[1]
    values = emission.shape[1]
    levels = lax.axis_size("leaf").bit_length() - 1
    place = lax.axis_index("leaf")
    weights = (
        mixing.astype(jnp.float32) / jnp.sum(mixing.astype(jnp.float32), axis=2, keepdims=True)
    ).astype(jnp.bfloat16)
    tables = (
        emission.astype(jnp.float32) / jnp.sum(emission.astype(jnp.float32), axis=1, keepdims=True)
    ).astype(jnp.bfloat16)
    prior_share = prior / jnp.sum(prior)
    onehots = (observed[:, :, None] == jnp.arange(values, dtype=jnp.int32)[None, None, :]).astype(
        jnp.bfloat16
    )
    emits = jnp.einsum("nrv,nvk->nrk", onehots, tables, preferred_element_type=jnp.float32)
    local_parent = parent - place * node_count
    prods = jnp.ones_like(emits)
    lam_list = [None] * node_count
    msg_list = [None] * node_count
    for node in range(node_count - 1, 0, -1):
        lam, msg = lift(emits[node] * prods[node], weights[node])
        lam_list[node] = lam
        msg_list[node] = msg
        slot = local_parent[node]
        current = lax.dynamic_index_in_dim(prods, slot, 0, keepdims=False)
        prods = lax.dynamic_update_index_in_dim(prods, current * msg, slot, 0)
    block_raw = emits[0] * prods[0]
    block_weight = weights[0]
    stored = []
    for level in range(levels):
        upper = jnp.bitwise_and(place, 1 << level) != 0
        other_raw = from_partner(block_raw, "leaf", level)
        other_weight = from_partner(block_weight, "leaf", level)
        child_raw = jnp.where(upper, block_raw, other_raw)
        child_weight = jnp.where(upper, block_weight, other_weight)
        child_lam, child_msg = lift(child_raw, child_weight)
        stored.append((child_lam, child_msg, child_weight))
        block_raw = jnp.where(upper, other_raw, block_raw) * child_msg
        block_weight = jnp.where(upper, other_weight, block_weight)
    top_lam, top_msg = lift(block_raw, block_weight)
    weighted = prior_share[None, :] * top_msg
    root_share = weighted / jnp.sum(weighted, axis=1, keepdims=True)
    top_ratio, top_post = settle(root_share, top_lam, top_msg, block_weight)
    for level in reversed(range(levels)):
        upper = jnp.bitwise_and(place, 1 << level) != 0
        child_lam, child_msg, child_weight = stored[level]
        ratio, post = settle(top_post, child_lam, child_msg, child_weight)
        top_lam = jnp.where(upper, child_lam, top_lam)
        top_ratio = jnp.where(upper, ratio, top_ratio)
        top_post = jnp.where(upper, post, top_post)
    lam_list[0] = top_lam
    posts = jnp.zeros_like(emits).at[0].set(top_post)
    ratio_list = [top_ratio] + [None] * (node_count - 1)
    for node in range(1, node_count):
        q_par = lax.dynamic_index_in_dim(posts, local_parent[node], 0, keepdims=False)
        ratio, post = settle(q_par, lam_list[node], msg_list[node], weights[node])
        ratio_list[node] = ratio
        posts = posts.at[node].set(post)
    ratio_all = jnp.stack(ratio_list, axis=0)
    lam_all = jnp.stack(lam_list, axis=0)
    post_half = posts.astype(jnp.bfloat16)
    emit_part = jnp.einsum("nrv,nrk->nvk", onehots, post_half, preferred_element_type=jnp.float32)
    groups = lax.axis_size("rows")
    share = states // groups
    spread = lax.all_to_all(ratio_all, "rows", split_axis=2, concat_axis=1, tiled=True)
    flows = jnp.einsum(
        "nra,nrb->nab",
        spread,
        lax.all_gather(lam_all, "rows", axis=1, tiled=True),
        preferred_element_type=jnp.float32,
    )
    emit_sum = sum_at_owner(emit_part.astype(jnp.bfloat16), "rows", 2)
    samples = row_count * groups
    own_rows = lax.dynamic_slice_in_dim(weights, lax.axis_index("rows") * share, share, 1)
    pair_counts = (own_rows.astype(jnp.float32) * flows * (states * states / samples)).astype(
        jnp.bfloat16
    )
    emit_counts = (emit_sum * (values * states / samples)).astype(jnp.bfloat16)
    return (pair_counts, emit_counts)


def solution(mesh):
    placed = (P("leaf", None, None), P("leaf", None, None), P(), P("leaf"), P("leaf", "rows"))
    return jax.shard_map(
        per_device,
        mesh=mesh,
        in_specs=placed,
        out_specs=(P("leaf", "rows", None), P("leaf", None, "rows")),
        check_vma=False,
    )
```

profile of v0, /device:TPU:8, one launch (start us, length us, event | category | flops | bytes accessed | tf_op | source)
XLA Modules:
  0.0 503.5 jit_solution(12902194291016919670)
XLA Ops:
  7.2 3.8 convert_reduce_fusion
  11.8 2.7 fusion
  14.5 2.6 copy-done
  17.4 1.7 convert_reduce_fusion.1
  19.1 2.5 collective-permute-done.1
  21.7 1.8 broadcast_select_fusion.10
  23.5 2.0 collective-permute-start.3
  29.3 1.9 fusion.6
  32.6 3.2 bitcast_dynamic-update-slice_fusion.1
  41.6 30.5 %collective-permute-done.3 = bf16[1024,1024]{1,0:T(8,128)(2,1)} collective-permute-done((bf16[1024,1024]{1,0:T(8,128)(2,1)S(1)}, bf16[1024,1024]{1,0:T(8,128)(2,1)}, u32[]{:S(2)}, u32[]{:S(2)}) %collective-permute-start.3) | collective-permute-done | bytes 2097184 | tf_op jit(solution)/shard_map/ppermute | solution.py:10
  73.7 3.3 collective-permute-start.5
  77.0 3.2 bitcast_dynamic-update-slice_fusion
  81.4 1.9 collective-permute-done
  83.6 3.9 select_multiply_fusion.5
  87.5 3.3 collective-permute-start.2
  90.8 77.3 %collective-permute-done.5 = bf16[1024,1024]{1,0:T(8,128)(2,1)} collective-permute-done((bf16[1024,1024]{1,0:T(8,128)(2,1)}, bf16[1024,1024]{1,0:T(8,128)(2,1)}, u32[]{:S(2)}, u32[]{:S(2)}) %collective-permute-start.5) | collective-permute-done | bytes 2097184 | tf_op jit(solution)/shard_map/ppermute | solution.py:10
  168.1 3.1 broadcast_select_fusion.6
  171.2 6.2 %collective-permute-start.7 = (bf16[1024,1024]{1,0:T(8,128)(2,1)}, bf16[1024,1024]{1,0:T(8,128)(2,1)}, u32[]{:S(2)}, u32[]{:S(2)}) collective-permute-start(bf16[1024,1024]{1,0:T(8,128)(2,1)} %broadcast_select_fusion.6), channel_id=1, source_target_pairs={{0,32},{4,36},{8,40},{12,44},{16,48},{20,52},{24,56},{28,60},{32,0... | collective-permute-start | bytes 6291464 | tf_op jit(solution)/shard_map/ppermute | solution.py:10
  177.7 3.2 select_multiply_fusion.4
  180.9 109.8 %collective-permute-done.4 = f32[128,1024]{1,0:T(8,128)S(1)} collective-permute-done((f32[128,1024]{1,0:T(8,128)S(1)}, f32[128,1024]{1,0:T(8,128)S(1)}, u32[]{:S(2)}, u32[]{:S(2)}) %collective-permute-start.4) | collective-permute-done | bytes 524320 | tf_op jit(solution)/shard_map/ppermute | solution.py:10
  290.9 3.1 broadcast_select_fusion.4
  294.6 3.3 select_multiply_fusion.3
  297.9 3.6 collective-permute-start.6
  301.5 25.1 %collective-permute-done.6 = f32[128,1024]{1,0:T(8,128)S(1)} collective-permute-done((f32[128,1024]{1,0:T(8,128)S(1)}, f32[128,1024]{1,0:T(8,128)S(1)}, u32[]{:S(2)}, u32[]{:S(2)}) %collective-permute-start.6) | collective-permute-done | bytes 524320 | tf_op jit(solution)/shard_map/ppermute | solution.py:10
  326.9 3.4 select_multiply_fusion.2
  331.9 11.0 %collective-permute-done.9 = bf16[1024,1024]{1,0:T(8,128)(2,1)} collective-permute-done((bf16[1024,1024]{1,0:T(8,128)(2,1)}, bf16[1024,1024]{1,0:T(8,128)(2,1)}, u32[]{:S(2)}, u32[]{:S(2)}) %collective-permute-start.9) | collective-permute-done | bytes 2097184 | tf_op jit(solution)/shard_map/ppermute | solution.py:10
  342.9 3.1 broadcast_select_fusion.2
  346.0 2.3 collective-permute-start.11
  348.3 5.7 %collective-permute-done.8 = f32[128,1024]{1,0:T(8,128)S(1)} collective-permute-done((f32[128,1024]{1,0:T(8,128)S(1)}, f32[128,1024]{1,0:T(8,128)S(1)}, u32[]{:S(2)}, u32[]{:S(2)}) %collective-permute-start.8) | collective-permute-done | bytes 524320 | tf_op jit(solution)/shard_map/ppermute | solution.py:10
  354.9 3.4 select_multiply_fusion.1
  358.4 2.3 collective-permute-start.10
  361.9 48.3 %collective-permute-done.10 = f32[128,1024]{1,0:T(8,128)S(1)} collective-permute-done((f32[128,1024]{1,0:T(8,128)S(1)}, f32[128,1024]{1,0:T(8,128)S(1)}, u32[]{:S(2)}, u32[]{:S(2)}) %collective-permute-start.10) | collective-permute-done | bytes 524320 | tf_op jit(solution)/shard_map/ppermute | solution.py:10
  410.6 3.4 fusion.45
  416.0 2.5 multiply_reduce_fusion
  418.6 2.3 divide_convert_fusion.5
  421.0 2.3 divide_convert_fusion.4
  423.3 2.3 divide_convert_fusion.3
  425.6 2.5 divide_convert_fusion.2
  428.2 2.4 divide_convert_fusion.1
  430.6 2.3 fusion.16
  433.9 2.2 select_bitcast_fusion
  437.3 1.7 fusion.10
  440.7 4.3 all-to-all-start
  445.0 2.1 fusion.13
  449.0 18.5 %all-to-all-done = bf16[3,128,1024]{1,0,2:T(4,128)(2,1)S(1)} async-done(((bf16[3,128,1024]{1,0,2:T(4,128)(2,1)}), bf16[3,128,1024]{1,0,2:T(4,128)(2,1)S(1)}, u32[]{:S(2)}, u32[]{:S(2)}) %all-to-all-start) | async-done | bytes 786464 | tf_op jit(solution)/shard_map/all_to_all | solution.py:105
  467.5 3.6 all-to-all-start.1
  474.3 16.8 %all-to-all-done.1 = bf16[4,3,256,256]{3,2,1,0:T(8,128)(2,1)S(1)} async-done(((bf16[4,3,256,256]{3,2,1,0:T(8,128)(2,1)}), bf16[4,3,256,256]{3,2,1,0:T(8,128)(2,1)S(1)}, u32[]{:S(2)}, u32[]{:S(2)}) %all-to-all-start.1) | async-done | bytes 1572896 | tf_op jit(solution)/shard_map/all_to_all | solution.py:21
  492.2 4.5 multiply_convert_fusion
  (133 shorter events, 28.3 us)
Async XLA Ops:
  7.2 485.0 %all-gather.2.cloned.1.call-start = ((), (), s32[]{:S(2)}) async-start(), calls=%async_computation.2 | async-start | bytes 3932160 | tf_op jit(solution)/shard_map/all_gather | solution.py:109
  7.2 4.6 copy-start.1
  14.5 2.6 copy-start
  17.1 2.0 copy-start.34
  17.3 4.4 collective-permute-start.1
  19.1 10.2 %copy-start.33 = (s32[3,128]{1,0:T(4,128)S(1)}, s32[3,128]{1,0:T(4,128)}, u32[]{:S(2)}) copy-start(s32[3,128]{1,0:T(4,128)} %param.15) | copy-start | bytes 4612
  23.5 48.7 %collective-permute-start.3 = (bf16[1024,1024]{1,0:T(8,128)(2,1)S(1)}, bf16[1024,1024]{1,0:T(8,128)(2,1)}, u32[]{:S(2)}, u32[]{:S(2)}) collective-permute-start(bf16[1024,1024]{1,0:T(8,128)(2,1)S(1)} %broadcast_select_fusion.10), channel_id=1, source_target_pairs={{0,8},{4,12},{8,0},{12,4},{16,24},{20,28},{24,16},{28,20},{32,40},... | collective-permute-start | bytes 6291464 | tf_op jit(solution)/shard_map/ppermute | solution.py:10
  31.2 1.2 copy-start.4
  32.4 3.4 copy-start.22
  35.8 1.2 copy-start.2
  41.6 35.4 %copy-start.12 = (bf16[1,128,1024]{2,1,0:T(8,128)(2,1)}, bf16[1,128,1024]{2,1,0:T(8,128)(2,1)S(1)}, u32[]{:S(2)}) copy-start(bf16[1,128,1024]{2,1,0:T(8,128)(2,1)S(1)} %get-tuple-element.50) | copy-start | bytes 786436
  41.6 35.4 %copy-start.8 = (f32[3,128,1024]{2,1,0:T(8,128)S(1)}, f32[3,128,1024]{2,1,0:T(8,128)}, u32[]{:S(2)}) copy-start(f32[3,128,1024]{2,1,0:T(8,128)} %copy.20) | copy-start | bytes 4718596
  73.7 94.4 %collective-permute-start.5 = (bf16[1024,1024]{1,0:T(8,128)(2,1)}, bf16[1024,1024]{1,0:T(8,128)(2,1)}, u32[]{:S(2)}, u32[]{:S(2)}) collective-permute-start(bf16[1024,1024]{1,0:T(8,128)(2,1)} %broadcast_select_fusion.8), channel_id=1, source_target_pairs={{0,16},{4,20},{8,24},{12,28},{16,0},{20,4},{24,8},{28,12},{32,48},... | collective-permute-start | bytes 6291464 | tf_op jit(solution)/shard_map/ppermute | solution.py:10
  81.3 2.0 collective-permute-start
  83.6 4.0 copy-start.9
  87.5 89.9 %collective-permute-start.2 = (f32[128,1024]{1,0:T(8,128)S(1)}, f32[128,1024]{1,0:T(8,128)S(1)}, u32[]{:S(2)}, u32[]{:S(2)}) collective-permute-start(f32[128,1024]{1,0:T(8,128)S(1)} %get-tuple-element.57), channel_id=1, source_target_pairs={{0,8},{4,12},{8,0},{12,4},{16,24},{20,28},{24,16},{28,20},{32,40},... | collective-permute-start | bytes 1572872 | tf_op jit(solution)/shard_map/ppermute | solution.py:10
  171.2 119.7 %collective-permute-start.7 = (bf16[1024,1024]{1,0:T(8,128)(2,1)}, bf16[1024,1024]{1,0:T(8,128)(2,1)}, u32[]{:S(2)}, u32[]{:S(2)}) collective-permute-start(bf16[1024,1024]{1,0:T(8,128)(2,1)} %broadcast_select_fusion.6), channel_id=1, source_target_pairs={{0,32},{4,36},{8,40},{12,44},{16,48},{20,52},{24,56},{28,60},{32,0... | collective-permute-start | bytes 6291464 | tf_op jit(solution)/shard_map/ppermute | solution.py:10
  180.9 109.8 %collective-permute-start.4 = (f32[128,1024]{1,0:T(8,128)S(1)}, f32[128,1024]{1,0:T(8,128)S(1)}, u32[]{:S(2)}, u32[]{:S(2)}) collective-permute-start(f32[128,1024]{1,0:T(8,128)S(1)} %get-tuple-element.59), channel_id=1, source_target_pairs={{0,16},{4,20},{8,24},{12,28},{16,0},{20,4},{24,8},{28,12},{32,48},... | collective-permute-start | bytes 1572872 | tf_op jit(solution)/shard_map/ppermute | solution.py:10
  294.0 48.8 %collective-permute-start.9 = (bf16[1024,1024]{1,0:T(8,128)(2,1)}, bf16[1024,1024]{1,0:T(8,128)(2,1)}, u32[]{:S(2)}, u32[]{:S(2)}) collective-permute-start(bf16[1024,1024]{1,0:T(8,128)(2,1)} %broadcast_select_fusion.4), channel_id=1, source_target_pairs={{0,64},{4,68},{8,72},{12,76},{16,80},{20,84},{24,88},{28,92},{32,9... | collective-permute-start | bytes 6291464 | tf_op jit(solution)/shard_map/ppermute | solution.py:10
  294.6 3.3 copy-start.5
  297.9 28.7 %collective-permute-start.6 = (f32[128,1024]{1,0:T(8,128)S(1)}, f32[128,1024]{1,0:T(8,128)S(1)}, u32[]{:S(2)}, u32[]{:S(2)}) collective-permute-start(f32[128,1024]{1,0:T(8,128)S(1)} %get-tuple-element.61), channel_id=1, source_target_pairs={{0,32},{4,36},{8,40},{12,44},{16,48},{20,52},{24,56},{28,60},{32,0... | collective-permute-start | bytes 1572872 | tf_op jit(solution)/shard_map/ppermute | solution.py:10
  326.9 3.4 copy-start.14
  330.3 23.7 %collective-permute-start.8 = (f32[128,1024]{1,0:T(8,128)S(1)}, f32[128,1024]{1,0:T(8,128)S(1)}, u32[]{:S(2)}, u32[]{:S(2)}) collective-permute-start(f32[128,1024]{1,0:T(8,128)S(1)} %get-tuple-element.63), channel_id=1, source_target_pairs={{0,64},{4,68},{8,72},{12,76},{16,80},{20,84},{24,88},{28,92},{32,9... | collective-permute-start | bytes 1572872 | tf_op jit(solution)/shard_map/ppermute | solution.py:10
  346.0 64.6 %collective-permute-start.11 = (bf16[1024,1024]{1,0:T(8,128)(2,1)}, bf16[1024,1024]{1,0:T(8,128)(2,1)}, u32[]{:S(2)}, u32[]{:S(2)}) collective-permute-start(bf16[1024,1024]{1,0:T(8,128)(2,1)} %broadcast_select_fusion.2), channel_id=1, source_target_pairs={{0,128},{4,132},{8,136},{12,140},{16,144},{20,148},{24,152},{28,15... | collective-permute-start | bytes 6291464 | tf_op jit(solution)/shard_map/ppermute | solution.py:10
  354.9 3.4 copy-start.17
  354.9 5.7 %copy-start.32 = (f32[1024]{0:T(1024)S(1)}, f32[1024]{0:T(1024)}, u32[]{:S(2)}) copy-start(f32[1024]{0:T(1024)} %param.13) | copy-start | bytes 12292
  358.4 51.9 %collective-permute-start.10 = (f32[128,1024]{1,0:T(8,128)S(1)}, f32[128,1024]{1,0:T(8,128)S(1)}, u32[]{:S(2)}, u32[]{:S(2)}) collective-permute-start(f32[128,1024]{1,0:T(8,128)S(1)} %get-tuple-element.65), channel_id=1, source_target_pairs={{0,128},{4,132},{8,136},{12,140},{16,144},{20,148},{24,152},{28,15... | collective-permute-start | bytes 1572872 | tf_op jit(solution)/shard_map/ppermute | solution.py:10
  410.5 3.5 copy-start.20
  410.5 3.5 copy-start.6
  410.5 3.5 copy-start.10
  410.5 3.5 copy-start.15
  410.5 3.5 copy-start.18
  416.0 2.5 copy-start.27
  418.6 2.4 copy-start.21
  418.6 2.4 copy-start.31
  420.9 2.3 copy-start.19
  421.0 2.3 copy-start.30
  423.3 2.3 copy-start.16
  423.3 2.3 copy-start.29
  425.6 2.5 copy-start.7
  425.6 2.5 copy-start.28
  428.2 5.5 %slice-start = ((s8[6291456]{0:T(1024)(128)(4,1)}), s8[4194304]{0:T(1024)(128)(4,1)S(1)}, s32[]{:S(2)}) async-start(s8[6291456]{0:T(1024)(128)(4,1)} %bitcast.126), calls=%async_computation.3 | async-start | bytes 8388608
  430.6 2.3 copy-start.26
  430.6 3.0 slice-start.1
  436.1 1.1 copy-start.24
  437.3 1.8 copy-start.25
  440.7 26.8 %all-to-all-start = ((bf16[3,128,1024]{1,0,2:T(4,128)(2,1)}), bf16[3,128,1024]{1,0,2:T(4,128)(2,1)S(1)}, u32[]{:S(2)}, u32[]{:S(2)}) async-start(bf16[3,128,1024]{1,0,2:T(4,128)(2,1)} %copy.10), calls=%async_computation | async-start | bytes 2097152 | tf_op jit(solution)/shard_map/all_to_all | solution.py:105
  467.5 23.7 %all-to-all-start.1 = ((bf16[4,3,256,256]{3,2,1,0:T(8,128)(2,1)}), bf16[4,3,256,256]{3,2,1,0:T(8,128)(2,1)S(1)}, u32[]{:S(2)}, u32[]{:S(2)}) async-start(bf16[4,3,256,256]{3,2,1,0:T(8,128)(2,1)} %bitcast.124), calls=%async_computation.1 | async-start | bytes 3145728 | tf_op jit(solution)/shard_map/all_to_all | solution.py:21
  (4 other events, 3.8 us)
Sparse Core Ops, SparseCore 0:
  416.1 48.4 all-gather.1
where the time goes:
time: 505 us; the launch traced here: 504 us
  waiting for transfers between devices  347 us (69%)
  matrix products  56.8 us (11%)
  starting transfers between devices  33.1 us (7%)
  other arithmetic  31.1 us (6%)
  between operations  18.7 us (4%)
  local copies, waits for them, and re-layouts  16.4 us (3%)
    ppermute x12, waiting for transfers between devices, from_partner(): return lax.ppermute(value, axis, pairs)  312 us
    dot_general x9, matrix products, lift(): lax.dot_general(lam, weight, (((1,), (1,)), ((), ())), preferred_element_...  29.7 us
    ppermute x12, starting transfers between devices, from_partner(): return lax.ppermute(value, axis, pairs)  25.2 us
    dot_general x9, matrix products, settle(): jnp.dot(ratio, weight, preferred_element_type=jnp.float32)  20.2 us
    all_to_all x1, waiting for transfers between devices, per_device(): lax.all_to_all(ratio_all, 'rows', split_axis=2, concat_axis=1, tiled=True)  18.5 us
    all_to_all x1, waiting for transfers between devices, sum_at_owner(): lax.all_to_all(in_blocks(array, dim, count), axis, 0, 0, tiled=True)  16.8 us
    select_n x5, other arithmetic, per_device(): block_weight = jnp.where(upper, other_weight, block_weight)  12.7 us
  transfers between devices with their start and end apart: 15, of which 11 were waited for; matrix products, arithmetic and copies ran while one was open for 14% of the time, Pallas kernels for 0%

commit v1 on v0

--- a/solution.py
+++ b/solution.py
@@ -102,7 +102,12 @@
     emit_part = jnp.einsum("nrv,nrk->nvk", onehots, post_half, preferred_element_type=jnp.float32)
     groups = lax.axis_size("rows")
     share = states // groups
-    spread = lax.all_to_all(ratio_all, "rows", split_axis=2, concat_axis=1, tiled=True)
+    spread = jnp.concatenate(
+        lax.all_to_all(
+            jnp.stack(jnp.split(ratio_all, lax.axis_size("rows"), axis=2)), "rows", 0, 0
+        ),
+        axis=1,
+    )
     flows = jnp.einsum(
         "nra,nrb->nab",
         spread,

time: 505 us -> 501 us (level)
  no operation moved by 1% of the time
where the time goes in v1:
time: 501 us; the launch traced here: 499 us
  waiting for transfers between devices  346 us (69%)
  matrix products  56.9 us (11%)
  starting transfers between devices  33.1 us (7%)
  other arithmetic  32.2 us (6%)
  between operations  18.7 us (4%)
  local copies, waits for them, and re-layouts  12.8 us (3%)
    ppermute x12, waiting for transfers between devices, from_partner(): return lax.ppermute(value, axis, pairs)  312 us
    dot_general x9, matrix products, lift(): lax.dot_general(lam, weight, (((1,), (1,)), ((), ())), preferred_element_...  29.6 us
    ppermute x12, starting transfers between devices, from_partner(): return lax.ppermute(value, axis, pairs)  25.2 us
    dot_general x9, matrix products, settle(): jnp.dot(ratio, weight, preferred_element_type=jnp.float32)  20.2 us
    all_to_all x1, waiting for transfers between devices, sum_at_owner(): lax.all_to_all(in_blocks(array, dim, count), axis, 0, 0, tiled=True)  17.7 us
    all_to_all x1, waiting for transfers between devices, per_device(): lax.all_to_all(jnp.stack(jnp.split(ratio_all, lax.axis_size('rows'), axis...  16 us
    select_n x5, other arithmetic, per_device(): block_weight = jnp.where(upper, other_weight, block_weight)  12.7 us
  transfers between devices with their start and end apart: 15, of which 11 were waited for; matrix products, arithmetic and copies ran while one was open for 14% of the time, Pallas kernels for 0%

profile of v1, /device:TPU:8, one launch (start us, length us, event | category | flops | bytes accessed | tf_op | source)
XLA Modules:
  0.0 499.4 jit_solution(2121275131405130888)
XLA Ops:
  7.2 3.8 convert_reduce_fusion
  11.8 2.7 fusion
  14.5 2.6 copy-done
  17.4 1.7 convert_reduce_fusion.1
  19.1 2.5 collective-permute-done.1
  21.7 1.8 broadcast_select_fusion.10
  23.5 2.0 collective-permute-start.3
  29.3 1.9 fusion.6
  32.6 3.2 bitcast_dynamic-update-slice_fusion.1
  41.6 30.6 %collective-permute-done.3 = bf16[1024,1024]{1,0:T(8,128)(2,1)} collective-permute-done((bf16[1024,1024]{1,0:T(8,128)(2,1)S(1)}, bf16[1024,1024]{1,0:T(8,128)(2,1)}, u32[]{:S(2)}, u32[]{:S(2)}) %collective-permute-start.3) | collective-permute-done | bytes 2097184 | tf_op jit(solution)/shard_map/ppermute | solution.py:10
  73.7 3.3 collective-permute-start.5
  77.0 3.2 bitcast_dynamic-update-slice_fusion
  81.4 1.9 collective-permute-done
  83.6 4.0 select_multiply_fusion.5
  87.5 3.3 collective-permute-start.2
  90.9 77.3 %collective-permute-done.5 = bf16[1024,1024]{1,0:T(8,128)(2,1)} collective-permute-done((bf16[1024,1024]{1,0:T(8,128)(2,1)}, bf16[1024,1024]{1,0:T(8,128)(2,1)}, u32[]{:S(2)}, u32[]{:S(2)}) %collective-permute-start.5) | collective-permute-done | bytes 2097184 | tf_op jit(solution)/shard_map/ppermute | solution.py:10
  168.1 3.1 broadcast_select_fusion.6
  171.2 6.2 %collective-permute-start.7 = (bf16[1024,1024]{1,0:T(8,128)(2,1)}, bf16[1024,1024]{1,0:T(8,128)(2,1)}, u32[]{:S(2)}, u32[]{:S(2)}) collective-permute-start(bf16[1024,1024]{1,0:T(8,128)(2,1)} %broadcast_select_fusion.6), channel_id=1, source_target_pairs={{0,32},{4,36},{8,40},{12,44},{16,48},{20,52},{24,56},{28,60},{32,0... | collective-permute-start | bytes 6291464 | tf_op jit(solution)/shard_map/ppermute | solution.py:10
  177.7 3.2 select_multiply_fusion.4
  180.9 109.8 %collective-permute-done.4 = f32[128,1024]{1,0:T(8,128)S(1)} collective-permute-done((f32[128,1024]{1,0:T(8,128)S(1)}, f32[128,1024]{1,0:T(8,128)S(1)}, u32[]{:S(2)}, u32[]{:S(2)}) %collective-permute-start.4) | collective-permute-done | bytes 524320 | tf_op jit(solution)/shard_map/ppermute | solution.py:10
  290.9 3.1 broadcast_select_fusion.4
  294.6 3.3 select_multiply_fusion.3
  297.9 3.6 collective-permute-start.6
  301.5 25.1 %collective-permute-done.6 = f32[128,1024]{1,0:T(8,128)S(1)} collective-permute-done((f32[128,1024]{1,0:T(8,128)S(1)}, f32[128,1024]{1,0:T(8,128)S(1)}, u32[]{:S(2)}, u32[]{:S(2)}) %collective-permute-start.6) | collective-permute-done | bytes 524320 | tf_op jit(solution)/shard_map/ppermute | solution.py:10
  326.9 3.4 select_multiply_fusion.2
  331.9 11.0 %collective-permute-done.9 = bf16[1024,1024]{1,0:T(8,128)(2,1)} collective-permute-done((bf16[1024,1024]{1,0:T(8,128)(2,1)}, bf16[1024,1024]{1,0:T(8,128)(2,1)}, u32[]{:S(2)}, u32[]{:S(2)}) %collective-permute-start.9) | collective-permute-done | bytes 2097184 | tf_op jit(solution)/shard_map/ppermute | solution.py:10
  342.9 3.1 broadcast_select_fusion.2
  346.0 2.3 collective-permute-start.11
  348.3 5.7 %collective-permute-done.8 = f32[128,1024]{1,0:T(8,128)S(1)} collective-permute-done((f32[128,1024]{1,0:T(8,128)S(1)}, f32[128,1024]{1,0:T(8,128)S(1)}, u32[]{:S(2)}, u32[]{:S(2)}) %collective-permute-start.8) | collective-permute-done | bytes 524320 | tf_op jit(solution)/shard_map/ppermute | solution.py:10
  354.9 3.4 select_multiply_fusion.1
  358.4 2.3 collective-permute-start.10
  362.0 48.2 %collective-permute-done.10 = f32[128,1024]{1,0:T(8,128)S(1)} collective-permute-done((f32[128,1024]{1,0:T(8,128)S(1)}, f32[128,1024]{1,0:T(8,128)S(1)}, u32[]{:S(2)}, u32[]{:S(2)}) %collective-permute-start.10) | collective-permute-done | bytes 524320 | tf_op jit(solution)/shard_map/ppermute | solution.py:10
  410.6 3.4 fusion.45
  416.0 2.5 multiply_reduce_fusion
  418.6 2.3 divide_convert_fusion.5
  421.0 2.3 divide_convert_fusion.4
  423.3 2.3 divide_convert_fusion.3
  425.7 2.5 divide_convert_fusion.2
  428.2 2.4 divide_convert_fusion.1
  430.6 2.3 fusion.16
  433.9 2.2 select_bitcast_fusion
  437.3 1.7 fusion.10
  440.3 4.3 all-to-all-start
  444.6 2.1 fusion.13
  448.6 16.0 %all-to-all-done = bf16[4,3,128,256]{3,2,1,0:T(8,128)(2,1)S(1)} async-done(((bf16[4,3,128,256]{3,2,1,0:T(8,128)(2,1)}), bf16[4,3,128,256]{3,2,1,0:T(8,128)(2,1)S(1)}, u32[]{:S(2)}, u32[]{:S(2)}) %all-to-all-start) | async-done | bytes 786464 | tf_op jit(solution)/shard_map/all_to_all | solution.py:106
  464.7 3.6 all-to-all-start.1
  469.2 17.7 %all-to-all-done.1 = bf16[4,3,256,256]{3,2,1,0:T(8,128)(2,1)S(1)} async-done(((bf16[4,3,256,256]{3,2,1,0:T(8,128)(2,1)}), bf16[4,3,256,256]{3,2,1,0:T(8,128)(2,1)S(1)}, u32[]{:S(2)}, u32[]{:S(2)}) %all-to-all-start.1) | async-done | bytes 1572896 | tf_op jit(solution)/shard_map/all_to_all | solution.py:21
  488.0 4.6 multiply_convert_fusion
  (135 shorter events, 25.8 us)
Async XLA Ops:
  7.2 480.8 %all-gather.2.cloned.1.call-start = ((), (), s32[]{:S(2)}) async-start(), calls=%async_computation.2 | async-start | bytes 3932160 | tf_op jit(solution)/shard_map/all_gather | solution.py:114
  7.2 4.6 copy-start.1
  14.5 2.6 copy-start
  17.1 2.0 copy-start.35
  17.3 4.4 collective-permute-start.1
  19.1 10.2 %copy-start.34 = (s32[3,128]{1,0:T(4,128)S(1)}, s32[3,128]{1,0:T(4,128)}, u32[]{:S(2)}) copy-start(s32[3,128]{1,0:T(4,128)} %param.15) | copy-start | bytes 4612
  23.5 48.7 %collective-permute-start.3 = (bf16[1024,1024]{1,0:T(8,128)(2,1)S(1)}, bf16[1024,1024]{1,0:T(8,128)(2,1)}, u32[]{:S(2)}, u32[]{:S(2)}) collective-permute-start(bf16[1024,1024]{1,0:T(8,128)(2,1)S(1)} %broadcast_select_fusion.10), channel_id=1, source_target_pairs={{0,8},{4,12},{8,0},{12,4},{16,24},{20,28},{24,16},{28,20},{32,40},... | collective-permute-start | bytes 6291464 | tf_op jit(solution)/shard_map/ppermute | solution.py:10
  31.2 1.1 copy-start.4
  32.4 3.4 copy-start.22
  35.8 1.2 copy-start.2
  41.6 35.4 %copy-start.12 = (bf16[1,128,1024]{2,1,0:T(8,128)(2,1)}, bf16[1,128,1024]{2,1,0:T(8,128)(2,1)S(1)}, u32[]{:S(2)}) copy-start(bf16[1,128,1024]{2,1,0:T(8,128)(2,1)S(1)} %get-tuple-element.50) | copy-start | bytes 786436
  41.6 35.4 %copy-start.8 = (f32[3,128,1024]{2,1,0:T(8,128)S(1)}, f32[3,128,1024]{2,1,0:T(8,128)}, u32[]{:S(2)}) copy-start(f32[3,128,1024]{2,1,0:T(8,128)} %copy.21) | copy-start | bytes 4718596
  73.7 94.4 %collective-permute-start.5 = (bf16[1024,1024]{1,0:T(8,128)(2,1)}, bf16[1024,1024]{1,0:T(8,128)(2,1)}, u32[]{:S(2)}, u32[]{:S(2)}) collective-permute-start(bf16[1024,1024]{1,0:T(8,128)(2,1)} %broadcast_select_fusion.8), channel_id=1, source_target_pairs={{0,16},{4,20},{8,24},{12,28},{16,0},{20,4},{24,8},{28,12},{32,48},... | collective-permute-start | bytes 6291464 | tf_op jit(solution)/shard_map/ppermute | solution.py:10
  81.3 2.0 collective-permute-start
  83.6 4.0 copy-start.9
  87.5 89.9 %collective-permute-start.2 = (f32[128,1024]{1,0:T(8,128)S(1)}, f32[128,1024]{1,0:T(8,128)S(1)}, u32[]{:S(2)}, u32[]{:S(2)}) collective-permute-start(f32[128,1024]{1,0:T(8,128)S(1)} %get-tuple-element.61), channel_id=1, source_target_pairs={{0,8},{4,12},{8,0},{12,4},{16,24},{20,28},{24,16},{28,20},{32,40},... | collective-permute-start | bytes 1572872 | tf_op jit(solution)/shard_map/ppermute | solution.py:10
  171.2 119.7 %collective-permute-start.7 = (bf16[1024,1024]{1,0:T(8,128)(2,1)}, bf16[1024,1024]{1,0:T(8,128)(2,1)}, u32[]{:S(2)}, u32[]{:S(2)}) collective-permute-start(bf16[1024,1024]{1,0:T(8,128)(2,1)} %broadcast_select_fusion.6), channel_id=1, source_target_pairs={{0,32},{4,36},{8,40},{12,44},{16,48},{20,52},{24,56},{28,60},{32,0... | collective-permute-start | bytes 6291464 | tf_op jit(solution)/shard_map/ppermute | solution.py:10
  180.9 109.8 %collective-permute-start.4 = (f32[128,1024]{1,0:T(8,128)S(1)}, f32[128,1024]{1,0:T(8,128)S(1)}, u32[]{:S(2)}, u32[]{:S(2)}) collective-permute-start(f32[128,1024]{1,0:T(8,128)S(1)} %get-tuple-element.63), channel_id=1, source_target_pairs={{0,16},{4,20},{8,24},{12,28},{16,0},{20,4},{24,8},{28,12},{32,48},... | collective-permute-start | bytes 1572872 | tf_op jit(solution)/shard_map/ppermute | solution.py:10
  294.0 48.8 %collective-permute-start.9 = (bf16[1024,1024]{1,0:T(8,128)(2,1)}, bf16[1024,1024]{1,0:T(8,128)(2,1)}, u32[]{:S(2)}, u32[]{:S(2)}) collective-permute-start(bf16[1024,1024]{1,0:T(8,128)(2,1)} %broadcast_select_fusion.4), channel_id=1, source_target_pairs={{0,64},{4,68},{8,72},{12,76},{16,80},{20,84},{24,88},{28,92},{32,9... | collective-permute-start | bytes 6291464 | tf_op jit(solution)/shard_map/ppermute | solution.py:10
  294.6 3.3 copy-start.5
  297.9 28.7 %collective-permute-start.6 = (f32[128,1024]{1,0:T(8,128)S(1)}, f32[128,1024]{1,0:T(8,128)S(1)}, u32[]{:S(2)}, u32[]{:S(2)}) collective-permute-start(f32[128,1024]{1,0:T(8,128)S(1)} %get-tuple-element.65), channel_id=1, source_target_pairs={{0,32},{4,36},{8,40},{12,44},{16,48},{20,52},{24,56},{28,60},{32,0... | collective-permute-start | bytes 1572872 | tf_op jit(solution)/shard_map/ppermute | solution.py:10
  326.9 3.4 copy-start.14
  330.3 23.7 %collective-permute-start.8 = (f32[128,1024]{1,0:T(8,128)S(1)}, f32[128,1024]{1,0:T(8,128)S(1)}, u32[]{:S(2)}, u32[]{:S(2)}) collective-permute-start(f32[128,1024]{1,0:T(8,128)S(1)} %get-tuple-element.67), channel_id=1, source_target_pairs={{0,64},{4,68},{8,72},{12,76},{16,80},{20,84},{24,88},{28,92},{32,9... | collective-permute-start | bytes 1572872 | tf_op jit(solution)/shard_map/ppermute | solution.py:10
  346.0 64.6 %collective-permute-start.11 = (bf16[1024,1024]{1,0:T(8,128)(2,1)}, bf16[1024,1024]{1,0:T(8,128)(2,1)}, u32[]{:S(2)}, u32[]{:S(2)}) collective-permute-start(bf16[1024,1024]{1,0:T(8,128)(2,1)} %broadcast_select_fusion.2), channel_id=1, source_target_pairs={{0,128},{4,132},{8,136},{12,140},{16,144},{20,148},{24,152},{28,15... | collective-permute-start | bytes 6291464 | tf_op jit(solution)/shard_map/ppermute | solution.py:10
  354.9 3.4 copy-start.17
  354.9 5.7 %copy-start.33 = (f32[1024]{0:T(1024)S(1)}, f32[1024]{0:T(1024)}, u32[]{:S(2)}) copy-start(f32[1024]{0:T(1024)} %param.13) | copy-start | bytes 12292
  358.4 51.9 %collective-permute-start.10 = (f32[128,1024]{1,0:T(8,128)S(1)}, f32[128,1024]{1,0:T(8,128)S(1)}, u32[]{:S(2)}, u32[]{:S(2)}) collective-permute-start(f32[128,1024]{1,0:T(8,128)S(1)} %get-tuple-element.69), channel_id=1, source_target_pairs={{0,128},{4,132},{8,136},{12,140},{16,144},{20,148},{24,152},{28,15... | collective-permute-start | bytes 1572872 | tf_op jit(solution)/shard_map/ppermute | solution.py:10
  410.5 3.5 copy-start.20
  410.5 3.5 copy-start.6
  410.5 3.5 copy-start.10
  410.5 3.5 copy-start.15
  410.5 3.5 copy-start.18
  416.0 2.5 copy-start.28
  418.6 2.4 copy-start.21
  418.6 2.4 copy-start.32
  421.0 2.3 copy-start.19
  421.0 2.3 copy-start.31
  423.3 2.3 copy-start.16
  423.3 2.3 copy-start.30
  425.6 2.5 copy-start.7
  425.6 2.5 copy-start.29
  428.2 5.4 %slice-start = ((s8[6291456]{0:T(1024)(128)(4,1)}), s8[4194304]{0:T(1024)(128)(4,1)S(1)}, s32[]{:S(2)}) async-start(s8[6291456]{0:T(1024)(128)(4,1)} %bitcast.130), calls=%async_computation.3 | async-start | bytes 8388608
  430.6 2.3 copy-start.26
  430.6 3.0 slice-start.1
  437.3 1.7 copy-start.25
  440.3 24.3 %all-to-all-start = ((bf16[4,3,128,256]{3,2,1,0:T(8,128)(2,1)}), bf16[4,3,128,256]{3,2,1,0:T(8,128)(2,1)S(1)}, u32[]{:S(2)}, u32[]{:S(2)}) async-start(bf16[4,3,128,256]{3,2,1,0:T(8,128)(2,1)} %pad_maximum_fusion.1), calls=%async_computation | async-start | bytes 1572864 | tf_op jit(solution)/shard_map/all_to_all | solution.py:106
  464.7 22.2 %all-to-all-start.1 = ((bf16[4,3,256,256]{3,2,1,0:T(8,128)(2,1)}), bf16[4,3,256,256]{3,2,1,0:T(8,128)(2,1)S(1)}, u32[]{:S(2)}, u32[]{:S(2)}) async-start(bf16[4,3,256,256]{3,2,1,0:T(8,128)(2,1)} %bitcast.129), calls=%async_computation.1 | async-start | bytes 3145728 | tf_op jit(solution)/shard_map/all_to_all | solution.py:21
  469.2 18.8 %copy-start.27 = (bf16[3,4,128,256]{3,2,1,0:T(8,128)(2,1)S(1)}, bf16[3,4,128,256]{3,2,1,0:T(8,128)(2,1)}, u32[]{:S(2)}) copy-start(bf16[3,4,128,256]{3,2,1,0:T(8,128)(2,1)} %copy.12) | copy-start | bytes 2359300
  (5 other events, 4.8 us)
Sparse Core Ops, SparseCore 0:
  416.1 47.9 all-gather.1
